TPU v7x, 32 devices: a whole 2x2x4 slice. The times are simulated.
32 devices in a mesh: row: 2 (over x), col: 16 (over z, y, core).
Axes of the slice: x: 2, y: 2, z: 4, core: 2. Of those that a mesh axis runs over, the one named last changes fastest.
Arguments:
- features: bfloat16 [8192, 256], P(('row', 'col')), may hold values from -6 to 6
- weight: bfloat16 [256, 128], replicated, may hold values from -0.375 to 0.375
- tiles: bfloat16 [2, 16, 320, 128, 128], P('row', 'col'), may hold values from -0.0625 to 0.0625
- slot_tile_row: int32 [2, 16, 320], P('row', 'col'), may hold values from 0 to 3
- tile_cols: int32 [2, 16, 320], P('row', 'col'), may hold values from 0 to 31
- live_tiles: int32 [2, 16], P('row', 'col'), may hold values from 40 to 320, as said below
- cotangent: bfloat16 [8192, 128], P(('row', 'col')), may hold values from -6 to 6
Outputs:
- logits: bfloat16 [8192, 128], P(('row', 'col'))
- grad_features: bfloat16 [8192, 256], P(('row', 'col'))
- grad_weight: float32 [256, 128], replicated
Inputs may be any that keep to these rules, and one draw needn't show every extreme that they name: Slots of a block from live_tiles on are padding and not part of the adjacency; in every draw some block has all 320 slots live.
All inputs are finite; a program needn't handle non-finite values.
Results may differ from a plain program's by a relative error of at most 0.005.
Values may be sent and summed in bfloat16 or wider, within the bound.
A program may use at most 128 MiB of HBM per device.

v0:
```python
import math
import jax
import jax.numpy as jnp
from jax import lax
from jax.sharding import PartitionSpec as P


def per_device(features, weight, tiles, slot_tile_row, tile_cols, live_tiles, cotangent):
    tile_block = tiles[0, 0]
    slot_rows = slot_tile_row[0, 0]
    slot_cols = tile_cols[0, 0]
    live_count = live_tiles[0, 0]
    tile_extent = tile_block.shape[-1]
    slot_total = tile_block.shape[0]
    stretch_rows = features.shape[0]
    output_width = weight.shape[1]
    row_count = lax.axis_size("row")
    col_count = lax.axis_size("col")
    row_tiles = row_count * stretch_rows // tile_extent
    col_tiles = col_count * stretch_rows // tile_extent
    block_size = 64
    block_total = slot_total // block_size
    projected_group = jnp.dot(
        lax.all_gather(features, "col", axis=0, tiled=True),
        weight,
        preferred_element_type=jnp.float32,
    ).astype(jnp.bfloat16)
    proj_tiles = projected_group.reshape(col_tiles, tile_extent, output_width)

    def block_slice(first_slot):
        part_tiles = lax.dynamic_slice_in_dim(tile_block, first_slot, block_size, 0)
        part_rows = lax.dynamic_slice_in_dim(slot_rows, first_slot, block_size, 0)
        part_cols = lax.dynamic_slice_in_dim(slot_cols, first_slot, block_size, 0)
        live_mask = first_slot + jnp.arange(block_size, dtype=jnp.int32) < live_count
        return (part_tiles, part_rows, part_cols, live_mask)

    def forward_block(block_index, totals):
        part_tiles, part_rows, part_cols, live_mask = block_slice(block_index * block_size)
        inputs = proj_tiles[part_cols]
        products = jnp.einsum(
            "tab,tbf->taf", part_tiles, inputs, preferred_element_type=jnp.float32
        )
        segment_ids = jnp.where(live_mask, part_rows, row_tiles)
        summed = jax.ops.segment_sum(products, segment_ids, num_segments=row_tiles + 1)
        return totals + summed[:row_tiles]

    forward_totals = lax.fori_loop(
        0,
        block_total,
        forward_block,
        jnp.zeros((row_tiles, tile_extent, output_width), jnp.float32),
    )
    logits = lax.psum_scatter(
        forward_totals.reshape(row_tiles * tile_extent, output_width),
        "row",
        scatter_dimension=0,
        tiled=True,
    ).astype(jnp.bfloat16)
    cot_group = lax.all_gather(cotangent, "row", axis=0, tiled=True)
    cot_tiles = cot_group.reshape(row_tiles, tile_extent, output_width)

    def backward_block(block_index, totals):
        part_tiles, part_rows, part_cols, live_mask = block_slice(block_index * block_size)
        inputs = cot_tiles[part_rows]
        products = jnp.einsum(
            "tab,taf->tbf", part_tiles, inputs, preferred_element_type=jnp.float32
        )
        inside = live_mask & (part_cols >= 0) & (part_cols < col_tiles)
        segment_ids = jnp.where(inside, part_cols, col_tiles)
        summed = jax.ops.segment_sum(products, segment_ids, num_segments=col_tiles + 1)
        return totals + summed[:col_tiles]

    empty = jnp.zeros((col_tiles, tile_extent, output_width), jnp.float32)
    backward_totals = lax.fori_loop(0, block_total, backward_block, empty).reshape(
        col_tiles * tile_extent, output_width
    )
    back = lax.psum_scatter(backward_totals, "col", scatter_dimension=0, tiled=True)
    back_rounded = back.astype(jnp.bfloat16)
    grad_features = jnp.dot(back_rounded, weight.T, preferred_element_type=jnp.float32).astype(
        jnp.bfloat16
    )
    weight_term = lax.dot_general(
        features, back_rounded, (((0,), (0,)), ((), ())), preferred_element_type=jnp.float32
    )
    node_total = stretch_rows * row_count * col_count
    grad_weight = lax.psum(weight_term, ("row", "col")) / math.sqrt(node_total)
    return (logits, grad_features, grad_weight)


def solution(mesh):
    placed = (
        P(("row", "col"), None),
        P(),
        P("row", "col", None, None, None),
        P("row", "col", None),
        P("row", "col", None),
        P("row", "col"),
        P(("row", "col"), None),
    )
    return jax.shard_map(
        per_device,
        mesh=mesh,
        in_specs=placed,
        out_specs=(P(("row", "col"), None), P(("row", "col"), None), P()),
        check_vma=False,
    )
```

profile of v0, /device:TPU:0, one launch (start us, length us, event | category | flops | bytes accessed | tf_op | source)
XLA Modules:
  0.0 375.7 jit_solution(15768739046971264460)
XLA Ops:
  8.6 14.4 %copy.10 = bf16[1,1,320,128,128]{3,4,2,1,0:T(8,128)(2,1)} copy(bf16[1,1,320,128,128]{4,3,2,1,0:T(8,128)(2,1)} %param.13) | data formatting | bytes 20971520 | tf_op args[2]
  23.0 5.9 %all_gather.7 = bf16[512,128]{1,0:T(8,128)(2,1)S(1)} all-gather(bf16[256,128]{1,0:T(8,128)(2,1)S(1)} %copy-done.3), channel_id=1, replica_groups=mesh['row'=2,'col'=16] {'row'}, dimensions={0}, use_global_device_ids=true | all-gather | bytes 196608 | tf_op jit(solution)/shard_map/all_gather | solution.py:59
  28.9 90.2 %while.29 = (s32[]{:T(128)}, f32[32,128,128]{2,1,0:T(8,128)}, s32[]{:T(128)}, s32[320]{0:T(512)S(1)}, bf16[320,128,128]{1,2,0:T(8,128)(2,1)}, /*index=5*/s32[320...) while((s32[]{:T(128)}, f32[32,128,128]{2,1,0:T(8,128)}, ...), condition=%wide.region_6.7_spmd.clone, body=%wide.region_4.6_spmd.clone.sunk | while | flops 270534272 | bytes 33626048 | solution.py:74
  29.6 1.0 gather_fusion.1
  30.6 4.4 %fusion.25 = f32[64,128,128]{2,1,0:T(8,128)} fusion(bf16[64,128,128]{2,1,0:T(8,128)(2,1)S(1)} %gather_fusion.1, bf16[320,128,128]{1,2,0:T(8,128)(2,1)} %get-tuple-element.501, s32[]{:T(128)S(6)} %select_n.64), kind=kOutput, calls=%fused_computation.12.clone.1 | convolution fusion | flops 268435456 | bytes 8388612 | tf_op jit(solution)/shard_map/while/body/eval_jaxpr/tab,taf->tbf/dot_general | solution.py:65
  35.2 8.8 %scatter_fusion.1 = f32[33,128,128]{2,1,0:T(8,128)S(1)} fusion(f32[33,128,128]{2,1,0:T(8,128)S(1)} %broadcast.112, s32[64]{0:T(128)S(1)} %get-tuple-element.435, f32[64,128,128]{2,1,0:T(8,128)} %fusion.25), kind=kCustom, calls=%fused_computation.3.clone.clone.1 | custom fusion | flops 1048576 | bytes 12583168 | tf_op jit(solution)/shard_map/while/body/eval_jaxpr/scatter-add | solution.py:70
  44.0 1.6 slice_add_fusion.5
  46.4 1.0 gather_fusion.1
  47.4 4.4 %fusion.25 = f32[64,128,128]{2,1,0:T(8,128)} fusion(bf16[64,128,128]{2,1,0:T(8,128)(2,1)S(1)} %gather_fusion.1, bf16[320,128,128]{1,2,0:T(8,128)(2,1)} %get-tuple-element.501, s32[]{:T(128)S(6)} %select_n.64), kind=kOutput, calls=%fused_computation.12.clone.1 | convolution fusion | flops 268435456 | bytes 8388612 | tf_op jit(solution)/shard_map/while/body/eval_jaxpr/tab,taf->tbf/dot_general | solution.py:65
  52.0 8.8 %scatter_fusion.1 = f32[33,128,128]{2,1,0:T(8,128)S(1)} fusion(f32[33,128,128]{2,1,0:T(8,128)S(1)} %broadcast.112, s32[64]{0:T(128)S(1)} %get-tuple-element.435, f32[64,128,128]{2,1,0:T(8,128)} %fusion.25), kind=kCustom, calls=%fused_computation.3.clone.clone.1 | custom fusion | flops 1048576 | bytes 12583168 | tf_op jit(solution)/shard_map/while/body/eval_jaxpr/scatter-add | solution.py:70
  60.8 3.2 slice_add_fusion.5
  64.8 1.0 gather_fusion.1
  65.7 4.4 %fusion.25 = f32[64,128,128]{2,1,0:T(8,128)} fusion(bf16[64,128,128]{2,1,0:T(8,128)(2,1)S(1)} %gather_fusion.1, bf16[320,128,128]{1,2,0:T(8,128)(2,1)} %get-tuple-element.501, s32[]{:T(128)S(6)} %select_n.64), kind=kOutput, calls=%fused_computation.12.clone.1 | convolution fusion | flops 268435456 | bytes 8388612 | tf_op jit(solution)/shard_map/while/body/eval_jaxpr/tab,taf->tbf/dot_general | solution.py:65
  70.3 8.8 %scatter_fusion.1 = f32[33,128,128]{2,1,0:T(8,128)S(1)} fusion(f32[33,128,128]{2,1,0:T(8,128)S(1)} %broadcast.112, s32[64]{0:T(128)S(1)} %get-tuple-element.435, f32[64,128,128]{2,1,0:T(8,128)} %fusion.25), kind=kCustom, calls=%fused_computation.3.clone.clone.1 | custom fusion | flops 1048576 | bytes 12583168 | tf_op jit(solution)/shard_map/while/body/eval_jaxpr/scatter-add | solution.py:70
  79.2 3.2 slice_add_fusion.5
  83.1 1.0 gather_fusion.1
  84.1 4.4 %fusion.25 = f32[64,128,128]{2,1,0:T(8,128)} fusion(bf16[64,128,128]{2,1,0:T(8,128)(2,1)S(1)} %gather_fusion.1, bf16[320,128,128]{1,2,0:T(8,128)(2,1)} %get-tuple-element.501, s32[]{:T(128)S(6)} %select_n.64), kind=kOutput, calls=%fused_computation.12.clone.1 | convolution fusion | flops 268435456 | bytes 8388612 | tf_op jit(solution)/shard_map/while/body/eval_jaxpr/tab,taf->tbf/dot_general | solution.py:65
  88.7 8.8 %scatter_fusion.1 = f32[33,128,128]{2,1,0:T(8,128)S(1)} fusion(f32[33,128,128]{2,1,0:T(8,128)S(1)} %broadcast.112, s32[64]{0:T(128)S(1)} %get-tuple-element.435, f32[64,128,128]{2,1,0:T(8,128)} %fusion.25), kind=kCustom, calls=%fused_computation.3.clone.clone.1 | custom fusion | flops 1048576 | bytes 12583168 | tf_op jit(solution)/shard_map/while/body/eval_jaxpr/scatter-add | solution.py:70
  97.5 3.2 slice_add_fusion.5
  101.5 1.0 gather_fusion.1
  102.4 4.4 %fusion.25 = f32[64,128,128]{2,1,0:T(8,128)} fusion(bf16[64,128,128]{2,1,0:T(8,128)(2,1)S(1)} %gather_fusion.1, bf16[320,128,128]{1,2,0:T(8,128)(2,1)} %get-tuple-element.501, s32[]{:T(128)S(6)} %select_n.64), kind=kOutput, calls=%fused_computation.12.clone.1 | convolution fusion | flops 268435456 | bytes 8388612 | tf_op jit(solution)/shard_map/while/body/eval_jaxpr/tab,taf->tbf/dot_general | solution.py:65
  107.1 8.8 %scatter_fusion.1 = f32[33,128,128]{2,1,0:T(8,128)S(1)} fusion(f32[33,128,128]{2,1,0:T(8,128)S(1)} %broadcast.112, s32[64]{0:T(128)S(1)} %get-tuple-element.435, f32[64,128,128]{2,1,0:T(8,128)} %fusion.25), kind=kCustom, calls=%fused_computation.3.clone.clone.1 | custom fusion | flops 1048576 | bytes 12583168 | tf_op jit(solution)/shard_map/while/body/eval_jaxpr/scatter-add | solution.py:70
  115.9 3.2 slice_add_fusion.5
  119.9 62.9 %reduce-scatter.5.cloned.1.call-done = f32[256,128]{1,0:T(8,128)} async-done(((f32[4096,128]{1,0:T(8,128)}), f32[256,128]{1,0:T(8,128)}) %reduce-scatter.5.cloned.1.call-update) | async-done | bytes 131088 | tf_op jit(solution)/shard_map/reduce_scatter | solution.py:77
  182.8 1.8 convolution_bitcast_fusion
  184.6 40.8 %all-gather.2.cloned.1.call-done = bf16[4096,256]{1,0:T(8,128)(2,1)} async-done(((bf16[256,256]{1,0:T(8,128)(2,1)}), bf16[4096,256]{1,0:T(8,128)(2,1)}) %all-gather.2.cloned.1.call-update) | async-done | bytes 2097168 | tf_op jit(solution)/shard_map/all_gather | solution.py:24
  225.4 2.3 convolution_convert_fusion
  227.7 74.2 %while.28 = (s32[]{:T(128)}, f32[4,128,128]{2,1,0:T(8,128)S(1)}, s32[]{:T(128)}, s32[320]{0:T(512)S(1)}, bf16[320,128,128]{2,1,0:T(8,128)(2,1)}, /*index=5*/s32[...) while((s32[]{:T(128)}, f32[4,128,128]{2,1,0:T(8,128)S(1)}, ...), condition=%wide.region_2.3_spmd.clone, body=%wide.region_0.2_spmd.clone.sunk | while | flops 269616512 | bytes 26286016 | solution.py:47
  228.4 1.0 gather_fusion
  229.4 4.2 %fusion.22 = f32[64,128,128]{2,1,0:T(8,128)} fusion(bf16[64,128,128]{2,1,0:T(8,128)(2,1)S(1)} %gather_fusion, bf16[320,128,128]{2,1,0:T(8,128)(2,1)} %get-tuple-element.465, s32[]{:T(128)S(6)} %select_n.62), kind=kOutput, calls=%fused_computation.4.clone.1 | convolution fusion | flops 268435456 | bytes 8388612 | tf_op jit(solution)/shard_map/while/body/eval_jaxpr/tab,tbf->taf/dot_general | solution.py:40
  233.7 8.8 %scatter_fusion = f32[5,128,128]{2,1,0:T(8,128)S(1)} fusion(f32[5,128,128]{2,1,0:T(8,128)S(1)} %broadcast.105, s32[64]{0:T(128)S(1)} %get-tuple-element.426, f32[64,128,128]{2,1,0:T(8,128)} %fusion.22), kind=kCustom, calls=%fused_computation.2.clone.clone.1 | custom fusion | flops 1048576 | bytes 12583168 | tf_op jit(solution)/shard_map/while/body/eval_jaxpr/scatter-add | solution.py:44
  243.3 1.0 gather_fusion
  244.2 4.2 %fusion.22 = f32[64,128,128]{2,1,0:T(8,128)} fusion(bf16[64,128,128]{2,1,0:T(8,128)(2,1)S(1)} %gather_fusion, bf16[320,128,128]{2,1,0:T(8,128)(2,1)} %get-tuple-element.465, s32[]{:T(128)S(6)} %select_n.62), kind=kOutput, calls=%fused_computation.4.clone.1 | convolution fusion | flops 268435456 | bytes 8388612 | tf_op jit(solution)/shard_map/while/body/eval_jaxpr/tab,tbf->taf/dot_general | solution.py:40
  248.5 8.8 %scatter_fusion = f32[5,128,128]{2,1,0:T(8,128)S(1)} fusion(f32[5,128,128]{2,1,0:T(8,128)S(1)} %broadcast.105, s32[64]{0:T(128)S(1)} %get-tuple-element.426, f32[64,128,128]{2,1,0:T(8,128)} %fusion.22), kind=kCustom, calls=%fused_computation.2.clone.clone.1 | custom fusion | flops 1048576 | bytes 12583168 | tf_op jit(solution)/shard_map/while/body/eval_jaxpr/scatter-add | solution.py:44
  258.1 1.0 gather_fusion
  259.1 4.2 %fusion.22 = f32[64,128,128]{2,1,0:T(8,128)} fusion(bf16[64,128,128]{2,1,0:T(8,128)(2,1)S(1)} %gather_fusion, bf16[320,128,128]{2,1,0:T(8,128)(2,1)} %get-tuple-element.465, s32[]{:T(128)S(6)} %select_n.62), kind=kOutput, calls=%fused_computation.4.clone.1 | convolution fusion | flops 268435456 | bytes 8388612 | tf_op jit(solution)/shard_map/while/body/eval_jaxpr/tab,tbf->taf/dot_general | solution.py:40
  263.4 8.8 %scatter_fusion = f32[5,128,128]{2,1,0:T(8,128)S(1)} fusion(f32[5,128,128]{2,1,0:T(8,128)S(1)} %broadcast.105, s32[64]{0:T(128)S(1)} %get-tuple-element.426, f32[64,128,128]{2,1,0:T(8,128)} %fusion.22), kind=kCustom, calls=%fused_computation.2.clone.clone.1 | custom fusion | flops 1048576 | bytes 12583168 | tf_op jit(solution)/shard_map/while/body/eval_jaxpr/scatter-add | solution.py:44
  273.0 1.0 gather_fusion
  273.9 4.2 %fusion.22 = f32[64,128,128]{2,1,0:T(8,128)} fusion(bf16[64,128,128]{2,1,0:T(8,128)(2,1)S(1)} %gather_fusion, bf16[320,128,128]{2,1,0:T(8,128)(2,1)} %get-tuple-element.465, s32[]{:T(128)S(6)} %select_n.62), kind=kOutput, calls=%fused_computation.4.clone.1 | convolution fusion | flops 268435456 | bytes 8388612 | tf_op jit(solution)/shard_map/while/body/eval_jaxpr/tab,tbf->taf/dot_general | solution.py:40
  278.2 8.8 %scatter_fusion = f32[5,128,128]{2,1,0:T(8,128)S(1)} fusion(f32[5,128,128]{2,1,0:T(8,128)S(1)} %broadcast.105, s32[64]{0:T(128)S(1)} %get-tuple-element.426, f32[64,128,128]{2,1,0:T(8,128)} %fusion.22), kind=kCustom, calls=%fused_computation.2.clone.clone.1 | custom fusion | flops 1048576 | bytes 12583168 | tf_op jit(solution)/shard_map/while/body/eval_jaxpr/scatter-add | solution.py:44
  287.8 1.0 gather_fusion
  288.8 4.2 %fusion.22 = f32[64,128,128]{2,1,0:T(8,128)} fusion(bf16[64,128,128]{2,1,0:T(8,128)(2,1)S(1)} %gather_fusion, bf16[320,128,128]{2,1,0:T(8,128)(2,1)} %get-tuple-element.465, s32[]{:T(128)S(6)} %select_n.62), kind=kOutput, calls=%fused_computation.4.clone.1 | convolution fusion | flops 268435456 | bytes 8388612 | tf_op jit(solution)/shard_map/while/body/eval_jaxpr/tab,tbf->taf/dot_general | solution.py:40
  293.1 8.8 %scatter_fusion = f32[5,128,128]{2,1,0:T(8,128)S(1)} fusion(f32[5,128,128]{2,1,0:T(8,128)S(1)} %broadcast.105, s32[64]{0:T(128)S(1)} %get-tuple-element.426, f32[64,128,128]{2,1,0:T(8,128)} %fusion.22), kind=kCustom, calls=%fused_computation.2.clone.clone.1 | custom fusion | flops 1048576 | bytes 12583168 | tf_op jit(solution)/shard_map/while/body/eval_jaxpr/scatter-add | solution.py:44
  302.7 1.8 convolution_convert_fusion.1
  304.4 50.3 %all-reduce.2.cloned.1.call-done = f32[256,128]{0,1:T(8,128)} async-done(((f32[256,128]{0,1:T(8,128)}), f32[256,128]{0,1:T(8,128)}) %all-reduce.2.cloned.1.call-update) | async-done | bytes 131088 | tf_op jit(solution)/shard_map/psum | solution.py:86
  354.7 0.9 broadcast_multiply_fusion
  356.4 11.2 %reduce-scatter.3.cloned.1.call-done = f32[256,128]{1,0:T(8,128)} async-done(((f32[512,128]{1,0:T(8,128)}), f32[256,128]{1,0:T(8,128)}) %reduce-scatter.3.cloned.1.call-update) | async-done | bytes 131088 | tf_op jit(solution)/shard_map/reduce_scatter | solution.py:53
  367.6 1.5 convert_element_type.13
  (56 shorter events, 12.8 us)
Async XLA Ops:
  7.2 218.2 %copy-start = (bf16[256,128]{1,0:T(8,128)(2,1)S(1)}, bf16[256,128]{1,0:T(8,128)(2,1)}, u32[]{:S(2)}) copy-start(bf16[256,128]{1,0:T(8,128)(2,1)} %param.12) | copy-start | bytes 196612
  7.2 175.6 %reduce-scatter.5.cloned.1.call-start = ((), (), s32[]{:S(2)}) async-start(), calls=%async_computation.4 | async-start | bytes 2228224 | tf_op jit(solution)/shard_map/reduce_scatter | solution.py:77
  8.6 14.4 %copy-start.3 = (bf16[256,128]{1,0:T(8,128)(2,1)S(1)}, bf16[256,128]{1,0:T(8,128)(2,1)}, u32[]{:S(2)}) copy-start(bf16[256,128]{1,0:T(8,128)(2,1)} %param.17) | copy-start | bytes 196612
  119.1 63.7 %copy-start.2 = (bf16[256,256]{1,0:T(8,128)(2,1)S(1)}, bf16[256,256]{1,0:T(8,128)(2,1)}, u32[]{:S(2)}) copy-start(bf16[256,256]{1,0:T(8,128)(2,1)} %param.11) | copy-start | bytes 393220
  119.1 106.3 %all-gather.2.cloned.1.call-start = ((), (), s32[]{:S(2)}) async-start(), calls=%async_computation.2 | async-start | bytes 2228224 | tf_op jit(solution)/shard_map/all_gather | solution.py:24
  119.9 234.9 %all-reduce.2.cloned.1.call-start = ((), (), s32[]{:S(2)}) async-start(), calls=%async_computation.5 | async-start | bytes 262144 | tf_op jit(solution)/shard_map/psum | solution.py:86
  184.6 183.1 %reduce-scatter.3.cloned.1.call-start = ((), (), s32[]{:S(2)}) async-start(), calls=%async_computation.3 | async-start | bytes 393216 | tf_op jit(solution)/shard_map/reduce_scatter | solution.py:53
  301.9 0.7 copy-start.1
Sparse Core Ops, SparseCore 0:
  119.3 63.4 reduce-scatter.4
  185.0 40.3 all-gather.1
  231.5 123.1 all-reduce.1
  356.8 10.7 reduce-scatter.2
where the time goes:
time: 378 us; the launch traced here: 376 us
  waiting for transfers between devices  166 us (44%)
  other arithmetic  114 us (30%)
  matrix products  48.8 us (13%)
  local copies, waits for them, and re-layouts  26.7 us (7%)
  between operations  13.8 us (4%)
  blocking collectives  5.85 us (2%)
    reduce_scatter x1, waiting for transfers between devices, per_device(): lax.psum_scatter(backward_totals, 'col', scatter_dimension=0, tiled=True)  62.9 us
    psum x1, waiting for transfers between devices, per_device(): grad_weight = lax.psum(weight_term, ('row', 'col')) / math.sqrt(node_total)  50.3 us
    scatter-add x5, other arithmetic, backward_block(): jax.ops.segment_sum(products, segment_ids, num_segments=col_tiles + 1)  44 us
    scatter-add x5, other arithmetic, forward_block(): jax.ops.segment_sum(products, segment_ids, num_segments=row_tiles + 1)  43.9 us
    all_gather x1, waiting for transfers between devices, per_device(): lax.all_gather(features, 'col', axis=0, tiled=True)  40.8 us
    dot_general x5, matrix products, backward_block(): jnp.einsum('tab,taf->tbf', part_tiles, inputs, preferred_element_type=jnp...  21.9 us
    dot_general x5, matrix products, forward_block(): jnp.einsum('tab,tbf->taf', part_tiles, inputs, preferred_element_type=jnp...  21.1 us
    unnamed x10, local copies, waits for them, and re-layouts  15.9 us
  transfers between devices with their start and end apart: 4, of which 4 were waited for; matrix products, arithmetic and copies ran while one was open for 22% of the time, Pallas kernels for 0%

commit v1 on v0

--- a/solution.py
+++ b/solution.py
@@ -83,7 +83,7 @@
         features, back_rounded, (((0,), (0,)), ((), ())), preferred_element_type=jnp.float32
     )
     node_total = stretch_rows * row_count * col_count
-    grad_weight = lax.psum(weight_term, ("row", "col")) / math.sqrt(node_total)
+    grad_weight = lax.psum(lax.psum(weight_term, "col"), "row") / math.sqrt(node_total)
     return (logits, grad_features, grad_weight)
 
 

time: 378 us -> 418 us (1.11)
  waiting for transfers between devices: 166 us -> 205 us
    psum x1 -> x2, waiting for transfers between devices: 50.3 us -> 88.6 us  [the longest x1 88.6 us: per_device(): lax.psum(weight_term, 'col')]
    all_gather x1, waiting for transfers between devices: 40.8 us -> 45.1 us  [per_device(): lax.all_gather(features, 'col', axis=0, tiled=True)]
  transfers between devices with their start and end apart: 4 -> 5, of which waited for: 4 -> 4; matrix products, arithmetic and copies ran while one was open for 22% -> 19% of each run, Pallas kernels for 0% -> 0%
where the time goes in v1:
time: 418 us; the launch traced here: 415 us
  waiting for transfers between devices  205 us (49%)
  other arithmetic  114 us (27%)
  matrix products  48.8 us (12%)
  local copies, waits for them, and re-layouts  26.7 us (6%)
  between operations  13.8 us (3%)
  blocking collectives  5.85 us (1%)
    psum x1, waiting for transfers between devices, per_device(): lax.psum(weight_term, 'col')  88.6 us
    reduce_scatter x1, waiting for transfers between devices, per_device(): lax.psum_scatter(backward_totals, 'col', scatter_dimension=0, tiled=True)  63.6 us
    all_gather x1, waiting for transfers between devices, per_device(): lax.all_gather(features, 'col', axis=0, tiled=True)  45.1 us
    scatter-add x5, other arithmetic, backward_block(): jax.ops.segment_sum(products, segment_ids, num_segments=col_tiles + 1)  44 us
    scatter-add x5, other arithmetic, forward_block(): jax.ops.segment_sum(products, segment_ids, num_segments=row_tiles + 1)  43.9 us
    dot_general x5, matrix products, backward_block(): jnp.einsum('tab,taf->tbf', part_tiles, inputs, preferred_element_type=jnp...  21.9 us
    dot_general x5, matrix products, forward_block(): jnp.einsum('tab,tbf->taf', part_tiles, inputs, preferred_element_type=jnp...  21.1 us
    unnamed x10, local copies, waits for them, and re-layouts  15.9 us
  transfers between devices with their start and end apart: 5, of which 4 were waited for; matrix products, arithmetic and copies ran while one was open for 19% of the time, Pallas kernels for 0%

profile of v1, /device:TPU:0, one launch (start us, length us, event | category | flops | bytes accessed | tf_op | source)
XLA Modules:
  0.0 415.1 jit_solution(12953329961797786191)
XLA Ops:
  8.6 14.4 %copy.10 = bf16[1,1,320,128,128]{3,4,2,1,0:T(8,128)(2,1)} copy(bf16[1,1,320,128,128]{4,3,2,1,0:T(8,128)(2,1)} %param.13) | data formatting | bytes 20971520 | tf_op args[2]
  23.0 5.9 %all_gather.7 = bf16[512,128]{1,0:T(8,128)(2,1)S(1)} all-gather(bf16[256,128]{1,0:T(8,128)(2,1)S(1)} %copy-done.3), channel_id=1, replica_groups=mesh['row'=2,'col'=16] {'row'}, dimensions={0}, use_global_device_ids=true | all-gather | bytes 196608 | tf_op jit(solution)/shard_map/all_gather | solution.py:59
  28.9 90.2 %while.29 = (s32[]{:T(128)}, f32[32,128,128]{2,1,0:T(8,128)}, s32[]{:T(128)}, s32[320]{0:T(512)S(1)}, bf16[320,128,128]{1,2,0:T(8,128)(2,1)}, /*index=5*/s32[320...) while((s32[]{:T(128)}, f32[32,128,128]{2,1,0:T(8,128)}, ...), condition=%wide.region_6.7_spmd.clone, body=%wide.region_4.6_spmd.clone.sunk | while | flops 270534272 | bytes 33626048 | solution.py:74
  29.6 1.0 gather_fusion.1
  30.6 4.4 %fusion.25 = f32[64,128,128]{2,1,0:T(8,128)} fusion(bf16[64,128,128]{2,1,0:T(8,128)(2,1)S(1)} %gather_fusion.1, bf16[320,128,128]{1,2,0:T(8,128)(2,1)} %get-tuple-element.501, s32[]{:T(128)S(6)} %select_n.64), kind=kOutput, calls=%fused_computation.12.clone.1 | convolution fusion | flops 268435456 | bytes 8388612 | tf_op jit(solution)/shard_map/while/body/eval_jaxpr/tab,taf->tbf/dot_general | solution.py:65
  35.2 8.8 %scatter_fusion.1 = f32[33,128,128]{2,1,0:T(8,128)S(1)} fusion(f32[33,128,128]{2,1,0:T(8,128)S(1)} %broadcast.112, s32[64]{0:T(128)S(1)} %get-tuple-element.435, f32[64,128,128]{2,1,0:T(8,128)} %fusion.25), kind=kCustom, calls=%fused_computation.3.clone.clone.1 | custom fusion | flops 1048576 | bytes 12583168 | tf_op jit(solution)/shard_map/while/body/eval_jaxpr/scatter-add | solution.py:70
  44.0 1.6 slice_add_fusion.5
  46.4 1.0 gather_fusion.1
  47.4 4.4 %fusion.25 = f32[64,128,128]{2,1,0:T(8,128)} fusion(bf16[64,128,128]{2,1,0:T(8,128)(2,1)S(1)} %gather_fusion.1, bf16[320,128,128]{1,2,0:T(8,128)(2,1)} %get-tuple-element.501, s32[]{:T(128)S(6)} %select_n.64), kind=kOutput, calls=%fused_computation.12.clone.1 | convolution fusion | flops 268435456 | bytes 8388612 | tf_op jit(solution)/shard_map/while/body/eval_jaxpr/tab,taf->tbf/dot_general | solution.py:65
  52.0 8.8 %scatter_fusion.1 = f32[33,128,128]{2,1,0:T(8,128)S(1)} fusion(f32[33,128,128]{2,1,0:T(8,128)S(1)} %broadcast.112, s32[64]{0:T(128)S(1)} %get-tuple-element.435, f32[64,128,128]{2,1,0:T(8,128)} %fusion.25), kind=kCustom, calls=%fused_computation.3.clone.clone.1 | custom fusion | flops 1048576 | bytes 12583168 | tf_op jit(solution)/shard_map/while/body/eval_jaxpr/scatter-add | solution.py:70
  60.8 3.2 slice_add_fusion.5
  64.8 1.0 gather_fusion.1
  65.7 4.4 %fusion.25 = f32[64,128,128]{2,1,0:T(8,128)} fusion(bf16[64,128,128]{2,1,0:T(8,128)(2,1)S(1)} %gather_fusion.1, bf16[320,128,128]{1,2,0:T(8,128)(2,1)} %get-tuple-element.501, s32[]{:T(128)S(6)} %select_n.64), kind=kOutput, calls=%fused_computation.12.clone.1 | convolution fusion | flops 268435456 | bytes 8388612 | tf_op jit(solution)/shard_map/while/body/eval_jaxpr/tab,taf->tbf/dot_general | solution.py:65
  70.3 8.8 %scatter_fusion.1 = f32[33,128,128]{2,1,0:T(8,128)S(1)} fusion(f32[33,128,128]{2,1,0:T(8,128)S(1)} %broadcast.112, s32[64]{0:T(128)S(1)} %get-tuple-element.435, f32[64,128,128]{2,1,0:T(8,128)} %fusion.25), kind=kCustom, calls=%fused_computation.3.clone.clone.1 | custom fusion | flops 1048576 | bytes 12583168 | tf_op jit(solution)/shard_map/while/body/eval_jaxpr/scatter-add | solution.py:70
  79.2 3.2 slice_add_fusion.5
  83.1 1.0 gather_fusion.1
  84.1 4.4 %fusion.25 = f32[64,128,128]{2,1,0:T(8,128)} fusion(bf16[64,128,128]{2,1,0:T(8,128)(2,1)S(1)} %gather_fusion.1, bf16[320,128,128]{1,2,0:T(8,128)(2,1)} %get-tuple-element.501, s32[]{:T(128)S(6)} %select_n.64), kind=kOutput, calls=%fused_computation.12.clone.1 | convolution fusion | flops 268435456 | bytes 8388612 | tf_op jit(solution)/shard_map/while/body/eval_jaxpr/tab,taf->tbf/dot_general | solution.py:65
  88.7 8.8 %scatter_fusion.1 = f32[33,128,128]{2,1,0:T(8,128)S(1)} fusion(f32[33,128,128]{2,1,0:T(8,128)S(1)} %broadcast.112, s32[64]{0:T(128)S(1)} %get-tuple-element.435, f32[64,128,128]{2,1,0:T(8,128)} %fusion.25), kind=kCustom, calls=%fused_computation.3.clone.clone.1 | custom fusion | flops 1048576 | bytes 12583168 | tf_op jit(solution)/shard_map/while/body/eval_jaxpr/scatter-add | solution.py:70
  97.5 3.2 slice_add_fusion.5
  101.5 1.0 gather_fusion.1
  102.4 4.4 %fusion.25 = f32[64,128,128]{2,1,0:T(8,128)} fusion(bf16[64,128,128]{2,1,0:T(8,128)(2,1)S(1)} %gather_fusion.1, bf16[320,128,128]{1,2,0:T(8,128)(2,1)} %get-tuple-element.501, s32[]{:T(128)S(6)} %select_n.64), kind=kOutput, calls=%fused_computation.12.clone.1 | convolution fusion | flops 268435456 | bytes 8388612 | tf_op jit(solution)/shard_map/while/body/eval_jaxpr/tab,taf->tbf/dot_general | solution.py:65
  107.1 8.8 %scatter_fusion.1 = f32[33,128,128]{2,1,0:T(8,128)S(1)} fusion(f32[33,128,128]{2,1,0:T(8,128)S(1)} %broadcast.112, s32[64]{0:T(128)S(1)} %get-tuple-element.435, f32[64,128,128]{2,1,0:T(8,128)} %fusion.25), kind=kCustom, calls=%fused_computation.3.clone.clone.1 | custom fusion | flops 1048576 | bytes 12583168 | tf_op jit(solution)/shard_map/while/body/eval_jaxpr/scatter-add | solution.py:70
  115.9 3.2 slice_add_fusion.5
  119.2 63.6 %reduce-scatter.5.cloned.1.call-done = f32[256,128]{1,0:T(8,128)} async-done(((f32[4096,128]{1,0:T(8,128)}), f32[256,128]{1,0:T(8,128)}) %reduce-scatter.5.cloned.1.call-update) | async-done | bytes 131088 | tf_op jit(solution)/shard_map/reduce_scatter | solution.py:77
  182.8 1.8 convolution_bitcast_fusion
  185.4 88.6 %all-reduce.3.cloned.1.call-done = f32[256,128]{0,1:T(8,128)} async-done(((f32[256,128]{0,1:T(8,128)}), f32[256,128]{0,1:T(8,128)}) %all-reduce.3.cloned.1.call-update) | async-done | bytes 131088 | tf_op jit(solution)/shard_map/psum | solution.py:86
  274.1 45.1 %all-gather.2.cloned.1.call-done = bf16[4096,256]{1,0:T(8,128)(2,1)} async-done(((bf16[256,256]{1,0:T(8,128)(2,1)}), bf16[4096,256]{1,0:T(8,128)(2,1)}) %all-gather.2.cloned.1.call-update) | async-done | bytes 2097168 | tf_op jit(solution)/shard_map/all_gather | solution.py:24
  319.2 2.3 convolution_convert_fusion
  321.5 74.2 %while.28 = (s32[]{:T(128)}, f32[4,128,128]{2,1,0:T(8,128)S(1)}, s32[]{:T(128)}, s32[320]{0:T(512)S(1)}, bf16[320,128,128]{2,1,0:T(8,128)(2,1)}, /*index=5*/s32[...) while((s32[]{:T(128)}, f32[4,128,128]{2,1,0:T(8,128)S(1)}, ...), condition=%wide.region_2.3_spmd.clone, body=%wide.region_0.2_spmd.clone.sunk | while | flops 269616512 | bytes 26286016 | solution.py:47
  322.3 1.0 gather_fusion
  323.2 4.2 %fusion.22 = f32[64,128,128]{2,1,0:T(8,128)} fusion(bf16[64,128,128]{2,1,0:T(8,128)(2,1)S(1)} %gather_fusion, bf16[320,128,128]{2,1,0:T(8,128)(2,1)} %get-tuple-element.465, s32[]{:T(128)S(6)} %select_n.62), kind=kOutput, calls=%fused_computation.4.clone.1 | convolution fusion | flops 268435456 | bytes 8388612 | tf_op jit(solution)/shard_map/while/body/eval_jaxpr/tab,tbf->taf/dot_general | solution.py:40
  327.5 8.8 %scatter_fusion = f32[5,128,128]{2,1,0:T(8,128)S(1)} fusion(f32[5,128,128]{2,1,0:T(8,128)S(1)} %broadcast.105, s32[64]{0:T(128)S(1)} %get-tuple-element.426, f32[64,128,128]{2,1,0:T(8,128)} %fusion.22), kind=kCustom, calls=%fused_computation.2.clone.clone.1 | custom fusion | flops 1048576 | bytes 12583168 | tf_op jit(solution)/shard_map/while/body/eval_jaxpr/scatter-add | solution.py:44
  337.1 1.0 gather_fusion
  338.1 4.2 %fusion.22 = f32[64,128,128]{2,1,0:T(8,128)} fusion(bf16[64,128,128]{2,1,0:T(8,128)(2,1)S(1)} %gather_fusion, bf16[320,128,128]{2,1,0:T(8,128)(2,1)} %get-tuple-element.465, s32[]{:T(128)S(6)} %select_n.62), kind=kOutput, calls=%fused_computation.4.clone.1 | convolution fusion | flops 268435456 | bytes 8388612 | tf_op jit(solution)/shard_map/while/body/eval_jaxpr/tab,tbf->taf/dot_general | solution.py:40
  342.3 8.8 %scatter_fusion = f32[5,128,128]{2,1,0:T(8,128)S(1)} fusion(f32[5,128,128]{2,1,0:T(8,128)S(1)} %broadcast.105, s32[64]{0:T(128)S(1)} %get-tuple-element.426, f32[64,128,128]{2,1,0:T(8,128)} %fusion.22), kind=kCustom, calls=%fused_computation.2.clone.clone.1 | custom fusion | flops 1048576 | bytes 12583168 | tf_op jit(solution)/shard_map/while/body/eval_jaxpr/scatter-add | solution.py:44
  351.9 1.0 gather_fusion
  352.9 4.2 %fusion.22 = f32[64,128,128]{2,1,0:T(8,128)} fusion(bf16[64,128,128]{2,1,0:T(8,128)(2,1)S(1)} %gather_fusion, bf16[320,128,128]{2,1,0:T(8,128)(2,1)} %get-tuple-element.465, s32[]{:T(128)S(6)} %select_n.62), kind=kOutput, calls=%fused_computation.4.clone.1 | convolution fusion | flops 268435456 | bytes 8388612 | tf_op jit(solution)/shard_map/while/body/eval_jaxpr/tab,tbf->taf/dot_general | solution.py:40
  357.2 8.8 %scatter_fusion = f32[5,128,128]{2,1,0:T(8,128)S(1)} fusion(f32[5,128,128]{2,1,0:T(8,128)S(1)} %broadcast.105, s32[64]{0:T(128)S(1)} %get-tuple-element.426, f32[64,128,128]{2,1,0:T(8,128)} %fusion.22), kind=kCustom, calls=%fused_computation.2.clone.clone.1 | custom fusion | flops 1048576 | bytes 12583168 | tf_op jit(solution)/shard_map/while/body/eval_jaxpr/scatter-add | solution.py:44
  366.8 1.0 gather_fusion
  367.7 4.2 %fusion.22 = f32[64,128,128]{2,1,0:T(8,128)} fusion(bf16[64,128,128]{2,1,0:T(8,128)(2,1)S(1)} %gather_fusion, bf16[320,128,128]{2,1,0:T(8,128)(2,1)} %get-tuple-element.465, s32[]{:T(128)S(6)} %select_n.62), kind=kOutput, calls=%fused_computation.4.clone.1 | convolution fusion | flops 268435456 | bytes 8388612 | tf_op jit(solution)/shard_map/while/body/eval_jaxpr/tab,tbf->taf/dot_general | solution.py:40
  372.0 8.8 %scatter_fusion = f32[5,128,128]{2,1,0:T(8,128)S(1)} fusion(f32[5,128,128]{2,1,0:T(8,128)S(1)} %broadcast.105, s32[64]{0:T(128)S(1)} %get-tuple-element.426, f32[64,128,128]{2,1,0:T(8,128)} %fusion.22), kind=kCustom, calls=%fused_computation.2.clone.clone.1 | custom fusion | flops 1048576 | bytes 12583168 | tf_op jit(solution)/shard_map/while/body/eval_jaxpr/scatter-add | solution.py:44
  381.6 1.0 gather_fusion
  382.6 4.2 %fusion.22 = f32[64,128,128]{2,1,0:T(8,128)} fusion(bf16[64,128,128]{2,1,0:T(8,128)(2,1)S(1)} %gather_fusion, bf16[320,128,128]{2,1,0:T(8,128)(2,1)} %get-tuple-element.465, s32[]{:T(128)S(6)} %select_n.62), kind=kOutput, calls=%fused_computation.4.clone.1 | convolution fusion | flops 268435456 | bytes 8388612 | tf_op jit(solution)/shard_map/while/body/eval_jaxpr/tab,tbf->taf/dot_general | solution.py:40
  386.8 8.8 %scatter_fusion = f32[5,128,128]{2,1,0:T(8,128)S(1)} fusion(f32[5,128,128]{2,1,0:T(8,128)S(1)} %broadcast.105, s32[64]{0:T(128)S(1)} %get-tuple-element.426, f32[64,128,128]{2,1,0:T(8,128)} %fusion.22), kind=kCustom, calls=%fused_computation.2.clone.clone.1 | custom fusion | flops 1048576 | bytes 12583168 | tf_op jit(solution)/shard_map/while/body/eval_jaxpr/scatter-add | solution.py:44
  396.4 1.7 convolution_convert_fusion.1
  398.2 0.9 broadcast_multiply_fusion
  399.8 7.2 %reduce-scatter.3.cloned.1.call-done = f32[256,128]{1,0:T(8,128)} async-done(((f32[512,128]{1,0:T(8,128)}), f32[256,128]{1,0:T(8,128)}) %reduce-scatter.3.cloned.1.call-update) | async-done | bytes 131088 | tf_op jit(solution)/shard_map/reduce_scatter | solution.py:53
  407.1 1.5 convert_element_type.13
  (59 shorter events, 12.8 us)
Async XLA Ops:
  7.2 312.1 %copy-start = (bf16[256,128]{1,0:T(8,128)(2,1)S(1)}, bf16[256,128]{1,0:T(8,128)(2,1)}, u32[]{:S(2)}) copy-start(bf16[256,128]{1,0:T(8,128)(2,1)} %param.12) | copy-start | bytes 196612
  7.2 175.6 %reduce-scatter.5.cloned.1.call-start = ((), (), s32[]{:S(2)}) async-start(), calls=%async_computation.4 | async-start | bytes 2228224 | tf_op jit(solution)/shard_map/reduce_scatter | solution.py:77
  8.6 14.4 %copy-start.3 = (bf16[256,128]{1,0:T(8,128)(2,1)S(1)}, bf16[256,128]{1,0:T(8,128)(2,1)}, u32[]{:S(2)}) copy-start(bf16[256,128]{1,0:T(8,128)(2,1)} %param.17) | copy-start | bytes 196612
  119.1 63.7 %copy-start.2 = (bf16[256,256]{1,0:T(8,128)(2,1)S(1)}, bf16[256,256]{1,0:T(8,128)(2,1)}, u32[]{:S(2)}) copy-start(bf16[256,256]{1,0:T(8,128)(2,1)} %param.11) | copy-start | bytes 393220
  119.1 154.9 %all-reduce.3.cloned.1.call-start = ((), (), s32[]{:S(2)}) async-start(), calls=%async_computation.5 | async-start | bytes 262144 | tf_op jit(solution)/shard_map/psum | solution.py:86
  184.6 134.6 %all-gather.2.cloned.1.call-start = ((), (), s32[]{:S(2)}) async-start(), calls=%async_computation.2 | async-start | bytes 2228224 | tf_op jit(solution)/shard_map/all_gather | solution.py:24
  185.3 212.9 %all-reduce.5.cloned.1.call-start = ((), (), s32[]{:S(2)}) async-start(), calls=%async_computation.6 | async-start | bytes 262144 | tf_op jit(solution)/shard_map/psum | solution.py:86
  274.0 133.0 %reduce-scatter.3.cloned.1.call-start = ((), (), s32[]{:S(2)}) async-start(), calls=%async_computation.3 | async-start | bytes 393216 | tf_op jit(solution)/shard_map/reduce_scatter | solution.py:53
  395.7 0.7 copy-start.1
Sparse Core Ops, SparseCore 0:
  119.3 63.4 reduce-scatter.4
  186.8 87.1 all-reduce.2
  276.2 42.9 all-gather.1
  321.3 20.2 all-reduce.4
  396.5 10.4 reduce-scatter.2
